TPU v7x, 32 devices: a whole 2x2x4 slice. The times are simulated.
32 devices in a mesh: dp: 4 (over y, x), seq: 8 (over z, core).
Axes of the slice: x: 2, y: 2, z: 4, core: 2. Of those that a mesh axis runs over, the one named last changes fastest.
Arguments:
- queries: bfloat16 [4, 1024, 2048], P('dp', 'seq'), may hold values from -80 to 80
- block_memory: bfloat16 [4, 1024, 1792], P('dp', 'seq'), may hold values from -80 to 80
- neighbour_ids: int32 [4, 16, 128], P('dp', 'seq'), may hold values from 0 to 63999
- embedding: bfloat16 [896, 64000], P('seq'), may hold values from -6 to 6
- enc_query_w: bfloat16 [896, 896], P('dp'), may hold values from -0.1875 to 0.1875
- enc_out_w: bfloat16 [896, 896], P('dp'), may hold values from -0.1875 to 0.1875
- key_w: bfloat16 [896, 2048], P('dp'), may hold values from -0.1875 to 0.1875
- value_w: bfloat16 [896, 2048], P('dp'), may hold values from -0.1875 to 0.1875
- context_cot: bfloat16 [4, 1024, 2048], P('dp', 'seq'), may hold values from -6 to 6
Outputs:
- context: bfloat16 [4, 1024, 2048], P('dp', 'seq')
- query_grad: bfloat16 [4, 1024, 2048], P('dp', 'seq')
- memory_grad: bfloat16 [4, 1024, 1792], P('dp', 'seq')
All inputs are finite; a program needn't handle non-finite values.
Results may differ from a plain program's by a relative error of at most 0.035.
The roundings to bfloat16 on the way count: a program that leaves them out, or rounds other values in their place, can miss the bound.
Values may be sent and summed in bfloat16 or wider, within the bound.
A program may use at most 128 MiB of HBM per device.

v0:
```python
import jax
import jax.numpy as jnp
from jax import lax
from jax.sharding import PartitionSpec as P

HEAD = 128
BLOCK = 64


def from_behind(value, axis, steps):
    count = lax.axis_size(axis)
    first, last = (max(0, -steps), min(count, count - steps))
    return lax.ppermute(value, axis, [(source, source + steps) for source in range(first, last)])


def softmax_rows(scores):
    top = jnp.max(scores, axis=-1, keepdims=True)
    expo = jnp.exp(scores - top)
    return expo / jnp.sum(expo, axis=-1, keepdims=True)


def encode(embedded, memory, query_full, out_full):
    count, nbr, width = embedded.shape
    heads = width // HEAD
    flat = embedded.reshape(count * nbr, width)
    enc_queries = jnp.dot(flat, query_full, preferred_element_type=jnp.float32).astype(jnp.bfloat16)
    enc_queries = enc_queries.reshape(count, nbr, heads, HEAD)
    split = memory.reshape(count, BLOCK, 2, heads, HEAD)
    mem_key = split[:, :, 0]
    mem_value = split[:, :, 1]
    scores = jnp.einsum(
        "cnhd,cmhd->chnm", enc_queries, mem_key, preferred_element_type=jnp.float32
    ) * HEAD ** (-0.5)
    enc_probs = softmax_rows(scores)
    enc_weights = enc_probs.astype(jnp.bfloat16)
    attended = jnp.einsum(
        "chnm,cmhd->cnhd", enc_weights, mem_value, preferred_element_type=jnp.float32
    ).astype(jnp.bfloat16)
    mixed = jnp.dot(
        attended.reshape(count * nbr, width), out_full, preferred_element_type=jnp.float32
    )
    encoded = (flat.astype(jnp.float32) + mixed).astype(jnp.bfloat16)
    return (encoded, (enc_queries, mem_key, mem_value, enc_probs, enc_weights))


def encode_grad(encoded_grad, saved, out_full):
    enc_queries, mem_key, mem_value, enc_probs, enc_weights = saved
    count, nbr, heads, head = enc_queries.shape
    attended_grad = lax.dot_general(
        encoded_grad, out_full, (((1,), (1,)), ((), ())), preferred_element_type=jnp.float32
    )
    attended_grad = attended_grad.astype(jnp.bfloat16).reshape(count, nbr, heads, head)
    inner = jnp.einsum(
        "cnhd,cmhd->chnm", attended_grad, mem_value, preferred_element_type=jnp.float32
    )
    centred = inner - jnp.sum(enc_probs * inner, axis=-1, keepdims=True)
    enc_d_scores = (enc_probs * centred * HEAD ** (-0.5)).astype(jnp.bfloat16)
    key_part = jnp.einsum(
        "chnm,cnhd->cmhd", enc_d_scores, enc_queries, preferred_element_type=jnp.float32
    )
    value_part = jnp.einsum(
        "chnm,cnhd->cmhd", enc_weights, attended_grad, preferred_element_type=jnp.float32
    )
    both = jnp.stack([key_part, value_part], axis=2)
    return both.reshape(count * BLOCK, 2 * heads * head).astype(jnp.bfloat16)


def attend(group_q, group_k, group_v):
    scores = jnp.einsum(
        "cthd,cnhd->chtn", group_q, group_k, preferred_element_type=jnp.float32
    ) * HEAD ** (-0.5)
    probs = softmax_rows(scores)
    weights = probs.astype(jnp.bfloat16)
    ctx = jnp.einsum(
        "chtn,cnhd->cthd", weights, group_v, preferred_element_type=jnp.float32
    ).astype(jnp.bfloat16)
    return (ctx, probs, weights)


def attend_grad(group_q, group_k, group_v, group_c, probs, weights):
    d_probs = jnp.einsum("cthd,cnhd->chtn", group_c, group_v, preferred_element_type=jnp.float32)
    centred = d_probs - jnp.sum(probs * d_probs, axis=-1, keepdims=True)
    d_scores = (probs * centred * HEAD ** (-0.5)).astype(jnp.bfloat16)
    d_query = jnp.einsum(
        "chtn,cnhd->cthd", d_scores, group_k, preferred_element_type=jnp.float32
    ).astype(jnp.bfloat16)
    d_key = jnp.einsum("chtn,cthd->cnhd", d_scores, group_q, preferred_element_type=jnp.float32)
    d_value = jnp.einsum("chtn,cthd->cnhd", weights, group_c, preferred_element_type=jnp.float32)
    return (d_query, d_key, d_value)


def body(
    queries,
    block_memory,
    neighbour_ids,
    embedding,
    enc_query_w,
    enc_out_w,
    key_w,
    value_w,
    context_cot,
):
    query_rows = queries[0]
    memory_rows = block_memory[0]
    cot_rows = context_cot[0]
    tok_rows, width = query_rows.shape
    count = tok_rows // BLOCK
    heads = width // HEAD
    all_ids = lax.all_gather(neighbour_ids, "seq", axis=1, tiled=True)[0]
    nbr = all_ids.shape[1]
    looked = jnp.take(embedding, all_ids.reshape(-1), axis=1)
    columns = lax.all_to_all(looked, "seq", split_axis=1, concat_axis=0, tiled=True)
    embedded = columns.T.reshape(count, nbr, columns.shape[0])
    query_full, out_full, key_full, value_full = (
        lax.all_gather(enc_query_w, "dp", axis=0, tiled=True),
        lax.all_gather(enc_out_w, "dp", axis=0, tiled=True),
        lax.all_gather(key_w, "dp", axis=0, tiled=True),
        lax.all_gather(value_w, "dp", axis=0, tiled=True),
    )
    encoded, saved = encode(embedded, memory_rows, query_full, out_full)
    keys = jnp.dot(encoded, key_full, preferred_element_type=jnp.float32).astype(jnp.bfloat16)
    values = jnp.dot(encoded, value_full, preferred_element_type=jnp.float32).astype(jnp.bfloat16)
    keys, values = (keys.reshape(-1, nbr, heads, HEAD), values.reshape(-1, nbr, heads, HEAD))
    sent_q, sent_c = from_behind((query_rows[:BLOCK], cot_rows[:BLOCK]), "seq", -1)
    group_q = jnp.concatenate([query_rows[BLOCK - 1 :], sent_q[: BLOCK - 1]], axis=0).reshape(
        count, BLOCK, heads, HEAD
    )
    group_c = jnp.concatenate([cot_rows[BLOCK - 1 :], sent_c[: BLOCK - 1]], axis=0).reshape(
        count, BLOCK, heads, HEAD
    )
    ctx, probs, weights = attend(group_q, keys, values)
    d_query, key_sum, value_sum = attend_grad(group_q, keys, values, group_c, probs, weights)
    ctx_flat = ctx.reshape(tok_rows, width)
    grad_flat = d_query.reshape(tok_rows, width)
    back_c, back_q = from_behind(
        (ctx_flat[tok_rows - BLOCK :], grad_flat[tok_rows - BLOCK :]), "seq", 1
    )
    context = jnp.concatenate([back_c[1:], ctx_flat[: tok_rows - BLOCK + 1]], axis=0)
    query_grad = jnp.concatenate([back_q[1:], grad_flat[: tok_rows - BLOCK + 1]], axis=0)
    key_b = key_sum.astype(jnp.bfloat16).reshape(count * nbr, width)
    value_b = value_sum.astype(jnp.bfloat16).reshape(count * nbr, width)
    encoded_grad = lax.dot_general(
        key_b, key_full, (((1,), (1,)), ((), ())), preferred_element_type=jnp.float32
    )
    encoded_grad = encoded_grad + lax.dot_general(
        value_b, value_full, (((1,), (1,)), ((), ())), preferred_element_type=jnp.float32
    )
    memory_grad = encode_grad(encoded_grad.astype(jnp.bfloat16), saved, out_full)
    return (context[None], query_grad[None], memory_grad[None])


def solution(mesh):
    placed = (
        P("dp", "seq", None),
        P("dp", "seq", None),
        P("dp", "seq", None),
        P("seq", None),
        P("dp", None),
        P("dp", None),
        P("dp", None),
        P("dp", None),
        P("dp", "seq", None),
    )
    return jax.shard_map(
        body,
        mesh=mesh,
        in_specs=placed,
        out_specs=(P("dp", "seq", None), P("dp", "seq", None), P("dp", "seq", None)),
        check_vma=False,
    )
```

profile of v0, /device:TPU:0, one launch (start us, length us, event | category | flops | bytes accessed | tf_op | source)
XLA Modules:
  0.0 262.4 jit_solution(5695888418865266772)
XLA Ops:
  10.0 19.2 %copy.51 = bf16[112,64000]{0,1:T(8,128)(2,1)} copy(bf16[112,64000]{1,0:T(8,128)(2,1)} %param.12) | data formatting | bytes 28672000 | tf_op args[3]
  29.2 13.6 %all_gather.15 = s32[1,16,128]{2,0,1:T(1,128)S(1)} all-gather(s32[1,2,128]{2,0,1:T(1,128)S(1)} %bitcast.144), channel_id=1, replica_groups=mesh['dp'=4,'seq'=8] {'seq'}, dimensions={1}, use_global_device_ids=true | all-gather | bytes 9216 | tf_op jit(solution)/shard_map/all_gather | solution.py:109
  42.9 13.4 %gather_fusion = bf16[2048,112]{1,0:T(8,128)(2,1)S(1)} fusion(bf16[112,64000]{0,1:T(8,128)(2,1)} %copy.51, s32[2048]{0:T(1024)S(1)} %broadcast_clamp_fusion), kind=kCustom, calls=%fused_computation | custom fusion | bytes 925696 | tf_op jit(solution)/shard_map/jit(_take)/gather | solution.py:111
  58.5 3.5 %all-to-all-start = ((bf16[112,8,256]{2,0,1:T(8,128)(2,1)}), bf16[112,8,256]{2,0,1:T(8,128)(2,1)S(1)}, u32[]{:S(2)}, u32[]{:S(2)}) async-start(bf16[112,8,256]{2,0,1:T(8,128)(2,1)} %broadcast_select_fusion), calls=%async_computation | async-start | bytes 917504 | tf_op jit(solution)/shard_map/all_to_all | solution.py:112
  62.8 1.3 collective-permute-start
  64.1 1.3 collective-permute-start.2
  66.5 1.0 maximum_bitcast_fusion
  68.5 1.0 maximum_bitcast_fusion.2
  70.4 5.6 %all-to-all-done = bf16[112,8,256]{2,0,1:T(8,128)(2,1)S(1)} async-done(((bf16[112,8,256]{2,0,1:T(8,128)(2,1)}), bf16[112,8,256]{2,0,1:T(8,128)(2,1)S(1)}, u32[]{:S(2)}, u32[]{:S(2)}) %all-to-all-start) | async-done | bytes 458784 | tf_op jit(solution)/shard_map/all_to_all | solution.py:112
  76.3 2.1 convolution_convert_fusion.8
  80.7 1.1 copy.58
  81.8 2.1 fusion.15
  83.9 42.8 %all-gather.9.cloned.1.call-done = bf16[896,2048]{1,0:T(8,128)(2,1)} async-done(((bf16[224,2048]{1,0:T(8,128)(2,1)}), bf16[896,2048]{1,0:T(8,128)(2,1)}) %all-gather.9.cloned.1.call-update) | async-done | bytes 3670032 | tf_op jit(solution)/shard_map/all_gather | solution.py:118
  126.8 3.3 %fusion.8 = bf16[32,8,16,128]{3,1,2,0:T(8,128)(2,1)S(1)} fusion(bf16[256,896]{1,0:T(8,128)(2,1)S(1)} %fusion.15, bf16[896,2048]{1,0:T(8,128)(2,1)} %all-gather.9.cloned.1.call-done), kind=kOutput, calls=%fused_computation.13 | convolution fusion | flops 940048384 | bytes 5177344 | tf_op jit(solution)/shard_map/dot_general | solution.py:122
  130.3 46.4 %all-gather.11.cloned.1.call-done = bf16[896,2048]{1,0:T(8,128)(2,1)} async-done(((bf16[224,2048]{1,0:T(8,128)(2,1)}), bf16[896,2048]{1,0:T(8,128)(2,1)}) %all-gather.11.cloned.1.call-update) | async-done | bytes 3670032 | tf_op jit(solution)/shard_map/all_gather | solution.py:117
  176.7 3.4 %fusion.9 = bf16[32,8,16,128]{3,1,2,0:T(8,128)(2,1)S(1)} fusion(bf16[256,896]{1,0:T(8,128)(2,1)S(1)} %fusion.15, bf16[896,2048]{1,0:T(8,128)(2,1)} %all-gather.11.cloned.1.call-done), kind=kOutput, calls=%fused_computation.14 | convolution fusion | flops 940048384 | bytes 5177344 | tf_op jit(solution)/shard_map/dot_general | solution.py:121
  181.1 1.3 fusion.73
  182.5 4.4 %fusion.17 = bf16[2,64,16,128]{3,1,2,0:T(8,128)(2,1)} fusion(bf16[2,128,16,128]{3,2,1,0:T(8,128)(2,1)S(1)} %bitcast.123, f32[2,16,64]{2,1,0:T(8,128)S(1)} %get-tuple-element.7, f32[2,16,64,128]{3,2,1,0:T(8,128)S(1)} %convolution_multiply_fusion), kind=kOutput, calls=%fused_computation.30 | convolution fusion | flops 68159616 | bytes 2629632 | tf_op jit(solution)/shard_map/chtn,cnhd->cthd/dot_general | solution.py:74
  186.9 2.9 %fusion.38 = f32[2,16,64,128]{3,2,1,0:T(8,128)} fusion(bf16[2,128,16,128]{3,2,1,0:T(8,128)(2,1)S(1)} %bitcast.124, bf16[2,64,16,128]{3,2,1,0:T(8,128)(2,1)} %bitcast.131), kind=kOutput, calls=%fused_computation.52 | convolution fusion | flops 67108864 | bytes 2621440 | tf_op jit(solution)/shard_map/cthd,cnhd->chtn/dot_general | solution.py:81
  189.8 14.1 %fusion.18 = bf16[2,64,16,128]{3,1,2,0:T(8,128)(2,1)} fusion(f32[2,16,64,128]{3,2,1,0:T(8,128)} %fusion.38, bf16[2,128,16,128]{3,2,1,0:T(8,128)(2,1)S(1)} %bitcast.126, f32[2,16,64,128]{3,2,1,0:T(8,128)} %get-tuple-element.8, f32[2,16,64]{2,1,0:T(8,128)S(1)} %get-tuple-element.7), kind=kOutput, calls=%fused_computation.31 | convolution fusion | flops 69208192 | bytes 3678208 | tf_op jit(solution)/shard_map/chtn,cnhd->cthd/dot_general | solution.py:84
  203.9 14.0 %fusion.5 = bf16[2,128,16,128]{1,3,2,0:T(8,128)(2,1)S(1)} fusion(f32[2,16,64,128]{3,2,1,0:T(8,128)} %fusion.38, bf16[2,64,16,128]{3,2,1,0:T(8,128)(2,1)S(1)} %bitcast.130, f32[2,16,64,128]{3,2,1,0:T(8,128)} %get-tuple-element.8, f32[2,16,64]{2,1,0:T(8,128)S(1)} %get-tuple-element.7), kind=kOutput, calls=%fused_computation.10 | convolution fusion | flops 69470336 | bytes 3678208 | tf_op jit(solution)/shard_map/chtn,cthd->cnhd/dot_general | solution.py:87
  218.0 5.3 %fusion.6 = bf16[2,128,16,128]{1,3,2,0:T(8,128)(2,1)} fusion(bf16[2,64,16,128]{3,2,1,0:T(8,128)(2,1)S(1)} %bitcast.132, f32[2,16,64]{2,1,0:T(8,128)S(1)} %get-tuple-element.7, f32[2,16,64,128]{3,2,1,0:T(8,128)S(1)} %convolution_multiply_fusion), kind=kOutput, calls=%fused_computation.11 | convolution fusion | flops 68421760 | bytes 2629632 | tf_op jit(solution)/shard_map/chtn,cthd->cnhd/dot_general | solution.py:88
  224.2 2.3 collective-permute-start.1
  227.4 3.9 %collective-permute-start.3 = (bf16[64,2048]{1,0:T(8,128)(2,1)}, bf16[64,2048]{1,0:T(8,128)(2,1)}, u32[]{:S(2)}, u32[]{:S(2)}) collective-permute-start(bf16[64,2048]{1,0:T(8,128)(2,1)} %bitcast.119), channel_id=1, source_target_pairs={{0,1},{1,2},{2,3},{3,4},{4,5},{5,6},{6,7},{8,9},{9,10},{10,11},{11... | collective-permute-start | bytes 786440 | tf_op jit(solution)/shard_map/ppermute | solution.py:13
  231.3 1.7 copy.70
  233.0 1.7 copy.72
  234.6 4.7 %fusion.31 = f32[256,896]{1,0:T(8,128)} fusion(bf16[896,2048]{1,0:T(8,128)(2,1)} %all-gather.11.cloned.1.call-done, bf16[32,8,16,128]{3,2,1,0:T(8,128)(2,1)} %bitcast.140), kind=kOutput, calls=%fused_computation.46 | convolution fusion | flops 939524096 | bytes 5636096 | tf_op jit(solution)/shard_map/dot_general | solution.py:142
  239.4 5.0 %convolution_convert_fusion.7 = bf16[256,896]{1,0:T(8,128)(2,1)} fusion(bf16[896,896]{1,0:T(8,128)(2,1)S(1)} %copy-done.6, f32[256,896]{1,0:T(8,128)} %fusion.31, bf16[896,2048]{1,0:T(8,128)(2,1)} %all-gather.9.cloned.1.call-done, bf16[32,8,16,128]{3,2,1,0:T(8,128)(2,1)S(1)} %bitcast.139), kind=kOutput, calls=%fused_computation.28 | convolution fusion | flops 1351254016 | bytes 7700480 | tf_op jit(solution)/shard_map/dot_general | solution.py:49
  244.4 1.5 reshape.126
  246.4 1.6 fusion.28
  247.9 1.4 fusion.27
  250.8 1.3 convert_element_type.99
  (93 shorter events, 20.0 us)
Async XLA Ops:
  7.2 69.1 %all-gather.5.cloned.1.call-start = ((), (), s32[]{:S(2)}) async-start(), calls=%async_computation.1 | async-start | bytes 2007040 | tf_op jit(solution)/shard_map/all_gather | solution.py:115
  7.9 73.9 %all-gather.7.cloned.1.call-start = ((), (), s32[]{:S(2)}) async-start(), calls=%async_computation.2 | async-start | bytes 2007040 | tf_op jit(solution)/shard_map/all_gather | solution.py:116
  8.6 118.1 %all-gather.9.cloned.1.call-start = ((), (), s32[]{:S(2)}) async-start(), calls=%async_computation.3 | async-start | bytes 4587520 | tf_op jit(solution)/shard_map/all_gather | solution.py:118
  9.4 167.3 %all-gather.11.cloned.1.call-start = ((), (), s32[]{:S(2)}) async-start(), calls=%async_computation.4 | async-start | bytes 4587520 | tf_op jit(solution)/shard_map/all_gather | solution.py:117
  10.0 19.2 %copy-start.16 = (s32[1,2,128]{2,1,0:T(2,128)S(1)}, s32[1,2,128]{2,1,0:T(2,128)}, u32[]{:S(2)}) copy-start(s32[1,2,128]{2,1,0:T(2,128)} %param.11) | copy-start | bytes 3076
  29.2 32.8 %copy-start.13 = (bf16[1,128,2048]{2,1,0:T(8,128)(2,1)S(1)}, bf16[1,128,2048]{2,1,0:T(8,128)(2,1)}, u32[]{:S(2)}) copy-start(bf16[1,128,2048]{2,1,0:T(8,128)(2,1)} %param.9) | copy-start | bytes 1572868
  42.8 21.2 %copy-start.14 = (bf16[1,128,2048]{2,1,0:T(8,128)(2,1)S(1)}, bf16[1,128,2048]{2,1,0:T(8,128)(2,1)}, u32[]{:S(2)}) copy-start(bf16[1,128,2048]{2,1,0:T(8,128)(2,1)} %param.17) | copy-start | bytes 1572868
  42.8 22.7 %copy-start.15 = (bf16[1,128,1792]{2,1,0:T(8,128)(2,1)S(1)}, bf16[1,128,1792]{2,1,0:T(8,128)(2,1)}, u32[]{:S(2)}) copy-start(bf16[1,128,1792]{2,1,0:T(8,128)(2,1)} %param.10) | copy-start | bytes 1376260
  58.5 17.5 %all-to-all-start = ((bf16[112,8,256]{2,0,1:T(8,128)(2,1)}), bf16[112,8,256]{2,0,1:T(8,128)(2,1)S(1)}, u32[]{:S(2)}, u32[]{:S(2)}) async-start(bf16[112,8,256]{2,0,1:T(8,128)(2,1)} %broadcast_select_fusion), calls=%async_computation | async-start | bytes 917504 | tf_op jit(solution)/shard_map/all_to_all | solution.py:112
  62.8 3.8 %collective-permute-start = (bf16[64,2048]{1,0:T(8,128)(2,1)}, bf16[64,2048]{1,0:T(8,128)(2,1)}, u32[]{:S(2)}, u32[]{:S(2)}) collective-permute-start(bf16[64,2048]{1,0:T(8,128)(2,1)} %slice_bitcast_fusion.3), channel_id=1, source_target_pairs={{1,0},{2,1},{3,2},{4,3},{5,4},{6,5},{7,6},{9,8},{10,9},{11,10},{12... | collective-permute-start | bytes 786440 | tf_op jit(solution)/shard_map/ppermute | solution.py:13
  64.1 4.4 %collective-permute-start.2 = (bf16[64,2048]{1,0:T(8,128)(2,1)S(1)}, bf16[64,2048]{1,0:T(8,128)(2,1)}, u32[]{:S(2)}, u32[]{:S(2)}) collective-permute-start(bf16[64,2048]{1,0:T(8,128)(2,1)S(1)} %slice_bitcast_fusion.2), channel_id=1, source_target_pairs={{1,0},{2,1},{3,2},{4,3},{5,4},{6,5},{7,6},{9,8},{10,9},{11,10},{12... | collective-permute-start | bytes 786440 | tf_op jit(solution)/shard_map/ppermute | solution.py:13
  66.2 14.1 %copy-start.11 = (bf16[2,64,1,7,128]{4,3,2,1,0:T(8,128)(2,1)}, bf16[2,64,1,7,128]{4,3,2,1,0:T(8,128)(2,1)S(1)}, u32[]{:S(2)}) copy-start(bf16[2,64,1,7,128]{4,3,2,1,0:T(8,128)(2,1)S(1)} %get-tuple-element.4) | copy-start | bytes 688132
  79.0 5.0 %copy-start.3 = (bf16[2,128,7,128]{3,2,1,0:T(8,128)(2,1)}, bf16[2,128,7,128]{3,2,1,0:T(8,128)(2,1)S(1)}, u32[]{:S(2)}) copy-start(bf16[2,128,7,128]{3,2,1,0:T(8,128)(2,1)S(1)} %reshape.125) | copy-start | bytes 1376260
  79.4 47.4 %copy-start.5 = (f32[2,7,128,64]{2,3,1,0:T(8,128)}, f32[2,7,128,64]{2,3,1,0:T(8,128)S(1)}, u32[]{:S(2)}) copy-start(f32[2,7,128,64]{2,3,1,0:T(8,128)S(1)} %convolution_multiply_fusion.1) | copy-start | bytes 1376260
  176.7 3.6 %copy-start = (bf16[16,8,16,128]{3,2,1,0:T(8,128)(2,1)S(1)}, bf16[16,8,16,128]{3,2,1,0:T(8,128)(2,1)}, u32[]{:S(2)}) copy-start(bf16[16,8,16,128]{3,2,1,0:T(8,128)(2,1)} %copy.86) | copy-start | bytes 1572868
  189.8 14.1 %copy-start.1 = (bf16[16,8,16,128]{3,2,1,0:T(8,128)(2,1)S(1)}, bf16[16,8,16,128]{3,2,1,0:T(8,128)(2,1)}, u32[]{:S(2)}) copy-start(bf16[16,8,16,128]{3,2,1,0:T(8,128)(2,1)} %copy.86) | copy-start | bytes 1572868
  203.9 14.0 %copy-start.2 = (bf16[16,8,16,128]{3,2,1,0:T(8,128)(2,1)S(1)}, bf16[16,8,16,128]{3,2,1,0:T(8,128)(2,1)}, u32[]{:S(2)}) copy-start(bf16[16,8,16,128]{3,2,1,0:T(8,128)(2,1)} %copy.92) | copy-start | bytes 1572868
  218.0 5.3 %slice-start = ((bf16[2,64,16,128]{3,1,2,0:T(8,128)(2,1)}), bf16[1,64,16,128]{3,1,2,0:T(8,128)(2,1)S(1)}, s32[]{:S(2)}) async-start(bf16[2,64,16,128]{3,1,2,0:T(8,128)(2,1)} %fusion.17), calls=%async_computation.5 | async-start | bytes 524288 | tf_op jit(solution)/shard_map/slice | solution.py:136
  218.0 8.5 %slice-start.1 = ((bf16[2,64,16,128]{3,1,2,0:T(8,128)(2,1)}), bf16[1,64,16,128]{3,1,2,0:T(8,128)(2,1)S(1)}, s32[]{:S(2)}) async-start(bf16[2,64,16,128]{3,1,2,0:T(8,128)(2,1)} %fusion.18), calls=%async_computation.6 | async-start | bytes 524288 | tf_op jit(solution)/shard_map/slice | solution.py:136
  223.2 9.7 %copy-start.9 = (bf16[2,128,16,128]{1,3,2,0:T(8,128)(2,1)S(1)}, bf16[2,128,16,128]{1,3,2,0:T(8,128)(2,1)}, u32[]{:S(2)}) copy-start(bf16[2,128,16,128]{1,3,2,0:T(8,128)(2,1)} %fusion.6) | copy-start | bytes 3145732
  224.2 27.9 %collective-permute-start.1 = (bf16[64,2048]{1,0:T(8,128)(2,1)}, bf16[64,2048]{1,0:T(8,128)(2,1)}, u32[]{:S(2)}, u32[]{:S(2)}) collective-permute-start(bf16[64,2048]{1,0:T(8,128)(2,1)} %bitcast.120), channel_id=1, source_target_pairs={{0,1},{1,2},{2,3},{3,4},{4,5},{5,6},{6,7},{8,9},{9,10},{10,11},{11... | collective-permute-start | bytes 786440 | tf_op jit(solution)/shard_map/ppermute | solution.py:13
  227.4 26.6 %collective-permute-start.3 = (bf16[64,2048]{1,0:T(8,128)(2,1)}, bf16[64,2048]{1,0:T(8,128)(2,1)}, u32[]{:S(2)}, u32[]{:S(2)}) collective-permute-start(bf16[64,2048]{1,0:T(8,128)(2,1)} %bitcast.119), channel_id=1, source_target_pairs={{0,1},{1,2},{2,3},{3,4},{4,5},{5,6},{6,7},{8,9},{9,10},{10,11},{11... | collective-permute-start | bytes 786440 | tf_op jit(solution)/shard_map/ppermute | solution.py:13
  234.6 4.7 %copy-start.6 = (bf16[896,896]{1,0:T(8,128)(2,1)S(1)}, bf16[896,896]{1,0:T(8,128)(2,1)}, u32[]{:S(2)}) copy-start(bf16[896,896]{1,0:T(8,128)(2,1)} %all-gather.7.cloned.1.call-done) | copy-start | bytes 4816900
  234.6 4.7 %copy-start.10 = (bf16[2,128,16,128]{3,2,1,0:T(8,128)(2,1)S(1)}, bf16[2,128,16,128]{3,2,1,0:T(8,128)(2,1)}, u32[]{:S(2)}) copy-start(bf16[2,128,16,128]{3,2,1,0:T(8,128)(2,1)} %copy.72) | copy-start | bytes 3145732
  239.4 6.5 %copy-start.12 = (bf16[2,64,1,7,128]{4,3,2,1,0:T(8,128)(2,1)S(1)}, bf16[2,64,1,7,128]{4,3,2,1,0:T(8,128)(2,1)}, u32[]{:S(2)}) copy-start(bf16[2,64,1,7,128]{4,3,2,1,0:T(8,128)(2,1)} %copy-done.11) | copy-start | bytes 688132
  239.4 7.0 %copy-start.4 = (bf16[2,128,7,128]{3,2,1,0:T(8,128)(2,1)S(1)}, bf16[2,128,7,128]{3,2,1,0:T(8,128)(2,1)}, u32[]{:S(2)}) copy-start(bf16[2,128,7,128]{3,2,1,0:T(8,128)(2,1)} %copy-done.3) | copy-start | bytes 1376260
  245.9 3.5 %copy-start.7 = (bf16[2,64,16,128]{3,1,2,0:T(8,128)(2,1)S(1)}, bf16[2,64,16,128]{3,1,2,0:T(8,128)(2,1)}, u32[]{:S(2)}) copy-start(bf16[2,64,16,128]{3,1,2,0:T(8,128)(2,1)} %fusion.17) | copy-start | bytes 1572868
  246.3 3.4 %copy-start.8 = (bf16[2,64,16,128]{3,1,2,0:T(8,128)(2,1)S(1)}, bf16[2,64,16,128]{3,1,2,0:T(8,128)(2,1)}, u32[]{:S(2)}) copy-start(bf16[2,64,16,128]{3,1,2,0:T(8,128)(2,1)} %fusion.18) | copy-start | bytes 1572868
Sparse Core Ops, SparseCore 0:
  9.8 33.8 all-gather.4
  45.5 31.0 all-gather.6
  78.5 48.1 all-gather.8
  128.5 48.1 all-gather.10
where the time goes:
time: 264 us; the launch traced here: 262 us
  waiting for transfers between devices  97.8 us (37%)
  matrix products  66.3 us (25%)
  local copies, waits for them, and re-layouts  50.5 us (19%)
  between operations  14.2 us (5%)
  blocking collectives  13.6 us (5%)
  starting transfers between devices  12.3 us (5%)
  other arithmetic  7.63 us (3%)
    all_gather x1, waiting for transfers between devices, body(): lax.all_gather(key_w, 'dp', axis=0, tiled=True)  46.4 us
    all_gather x1, waiting for transfers between devices, body(): lax.all_gather(value_w, 'dp', axis=0, tiled=True)  42.8 us
    unnamed x43, local copies, waits for them, and re-layouts  23.4 us
    dot_general x1, matrix products, attend_grad(): jnp.einsum('chtn,cnhd->cthd', d_scores, group_k, preferred_element_type=j...  14.1 us
    dot_general x1, matrix products, attend_grad(): jnp.einsum('chtn,cthd->cnhd', d_scores, group_q, preferred_element_type=j...  14 us
    gather x2, local copies, waits for them, and re-layouts, body(): looked = jnp.take(embedding, all_ids.reshape(-1), axis=1)  13.6 us
    all_gather x1, blocking collectives, body(): all_ids = lax.all_gather(neighbour_ids, 'seq', axis=1, tiled=True)[0]  13.6 us
    ppermute x4, starting transfers between devices, from_behind(): lax.ppermute(value, axis, [(source, source + steps) for source in range(f...  8.71 us
  transfers between devices with their start and end apart: 9, of which 4 were waited for; matrix products, arithmetic and copies ran while one was open for 29% of the time, Pallas kernels for 0%

commit v1 on v0

v1 whole, which is shorter than its diff:
```python
import functools

import jax
import jax.numpy as jnp
from jax import lax
from jax.experimental import pallas as pl
from jax.experimental.pallas import tpu as pltpu
from jax.sharding import PartitionSpec as P

HEAD = 128
BLOCK = 64
SCALE = HEAD ** (-0.5)
F32 = jnp.float32
BF16 = jnp.bfloat16
MESH = pl.DeviceIdType.MESH


def ids_kernel(seqs, q_ref, c_ref, ids_ref, ids_out, halo_q, halo_c, send, recv, halo_send, halo_recv, local):
    dp = lax.axis_index("dp")
    sq = lax.axis_index("seq")
    own = pltpu.make_async_copy(ids_ref, ids_out.at[sq], local)
    own.start()
    barrier = pltpu.get_barrier_semaphore()
    for k in range(1, seqs):
        pl.semaphore_signal(
            barrier, inc=1, device_id=(dp, lax.rem(sq + k, seqs)), device_id_type=MESH
        )
    pl.semaphore_wait(barrier, seqs - 1)

    copies = []
    for k in range(1, seqs):
        copies.append(
            pltpu.make_async_remote_copy(
                src_ref=ids_ref,
                dst_ref=ids_out.at[sq],
                send_sem=send.at[k],
                recv_sem=recv.at[k],
                device_id=(dp, lax.rem(sq + k, seqs)),
                device_id_type=MESH,
            )
        )
        copies[-1].start()
    for i, (src, dst) in enumerate(((q_ref, halo_q), (c_ref, halo_c))):
        copies.append(
            pltpu.make_async_remote_copy(
                src_ref=src.at[pl.ds(0, BLOCK)],
                dst_ref=dst,
                send_sem=halo_send.at[i],
                recv_sem=halo_recv.at[i],
                device_id=(dp, lax.rem(sq + seqs - 1, seqs)),
                device_id_type=MESH,
            )
        )
        copies[-1].start()
    own.wait()
    for copy in copies:
        copy.wait()


def share_ids(q, c, ids):
    seqs = lax.axis_size("seq")
    anywhere = pl.BlockSpec(memory_space=pl.ANY)
    dma = pltpu.SemaphoreType.DMA
    shape = jax.ShapeDtypeStruct
    return pl.pallas_call(
        functools.partial(ids_kernel, seqs),
        out_shape=[
            shape((seqs,) + ids.shape, jnp.int32),
            shape((BLOCK, q.shape[1]), BF16),
            shape((BLOCK, q.shape[1]), BF16),
        ],
        in_specs=[anywhere] * 3,
        out_specs=[anywhere] * 3,
        scratch_shapes=[dma((seqs,)), dma((seqs,)), dma((2,)), dma((2,)), dma],
        compiler_params=pltpu.CompilerParams(collective_id=1, has_side_effects=True),
    )(q, c, ids)


def look_kernel(ids, table, out):
    seqs, count, nbr = ids.shape
    feats = table.shape[0]
    lane = lax.broadcasted_iota(jnp.int32, (feats, HEAD), 1)
    step = 8

    def chunk(to, carry):
        for b in range(count):
            for part in range(nbr // HEAD):

                def some(i, acc):
                    for t in range(step):
                        j = i * step + t
                        token = ids[to, b, part * HEAD + j]
                        start = pl.multiple_of((token >> 7) << 7, HEAD)
                        tile = table[:, pl.ds(start, HEAD)].astype(F32)
                        moved = pltpu.roll(tile, (j - token) & (HEAD - 1), 1)
                        acc = jnp.where(lane == j, moved, acc)
                    return acc

                acc = lax.fori_loop(0, HEAD // step, some, jnp.zeros((feats, HEAD), F32))
                first = b * nbr + part * HEAD
                out[to, :, first : first + HEAD] = acc.astype(BF16)
        return carry

    lax.fori_loop(0, seqs, chunk, 0)


def look_up(ids, table):
    seqs, count, nbr = ids.shape
    feats = table.shape[0]
    return pl.pallas_call(
        look_kernel,
        out_shape=jax.ShapeDtypeStruct((seqs, feats, count * nbr), BF16),
        in_specs=[
            pl.BlockSpec(memory_space=pltpu.SMEM),
            pl.BlockSpec(memory_space=pltpu.VMEM),
        ],
        out_specs=pl.BlockSpec(memory_space=pltpu.VMEM),
    )(ids, table)


def gather_kernel(
    dps,
    seqs,
    stage,
    eq_ref,
    eo_ref,
    kw_ref,
    vw_ref,
    emb_out,
    eq_out,
    eo_out,
    kw_out,
    vw_out,
    w_send,
    w_recv,
    fwd_send,
    emb_send,
    emb_recv,
    local,
):
    dp = lax.axis_index("dp")
    sq = lax.axis_index("seq")
    core = lax.rem(sq, 2)
    mate = sq + 1 - 2 * core
    weights = ((eq_ref, eq_out), (eo_ref, eo_out), (kw_ref, kw_out), (vw_ref, vw_out))
    own = [pltpu.make_async_copy(stage.at[sq], emb_out.at[sq], local.at[4])]
    for w, (src, dst) in enumerate(weights):
        own.append(pltpu.make_async_copy(src, dst.at[dp], local.at[w]))
    for copy in own:
        copy.start()

    barrier = pltpu.get_barrier_semaphore()
    for k in range(1, seqs):
        pl.semaphore_signal(
            barrier, inc=1, device_id=(dp, lax.rem(sq + k, seqs)), device_id_type=MESH
        )
    for k in range(1, dps):
        pl.semaphore_signal(
            barrier, inc=1, device_id=(lax.rem(dp + k, dps), sq), device_id_type=MESH
        )
    pl.semaphore_wait(barrier, seqs - 1 + dps - 1)

    def w_copy(w, to):
        src, dst = weights[w]
        return pltpu.make_async_remote_copy(
            src_ref=src,
            dst_ref=dst.at[dp],
            send_sem=w_send.at[w, to],
            recv_sem=w_recv.at[w, dp],
            device_id=(to, sq),
            device_id_type=MESH,
        )

    def w_forward(w, owner):
        dst = weights[w][1]
        return pltpu.make_async_remote_copy(
            src_ref=dst.at[owner],
            dst_ref=dst.at[owner],
            send_sem=fwd_send.at[w, owner],
            recv_sem=w_recv.at[w, owner],
            device_id=(dp, mate),
            device_id_type=MESH,
        )

    def emb_copy(to):
        return pltpu.make_async_remote_copy(
            src_ref=stage.at[to],
            dst_ref=emb_out.at[sq],
            send_sem=emb_send.at[to],
            recv_sem=emb_recv.at[sq],
            device_id=(dp, to),
            device_id_type=MESH,
        )

    def arrived(ref, sem):
        pltpu.make_async_copy(ref, ref, sem).wait()

    for side in range(2):

        @pl.when(core == side)
        def _():
            for w in (side, 2 + side):
                for k in range(1, dps):
                    w_copy(w, lax.rem(dp + k, dps)).start()

    for k in range(1, seqs):
        emb_copy(lax.rem(sq + k, seqs)).start()

    for side in range(2):

        @pl.when(core == side)
        def _():
            for w in (side, 2 + side):
                for k in range(1, dps):
                    owner = lax.rem(dp + k, dps)
                    arrived(weights[w][1].at[owner], w_recv.at[w, owner])
                    w_forward(w, owner).start()
            for w in (1 - side, 3 - side):
                for k in range(1, dps):
                    owner = lax.rem(dp + k, dps)
                    arrived(weights[w][1].at[owner], w_recv.at[w, owner])
            for w in (side, 2 + side):
                for k in range(1, dps):
                    w_copy(w, lax.rem(dp + k, dps)).wait_send()
                    w_forward(w, lax.rem(dp + k, dps)).wait_send()

    for copy in own:
        copy.wait()
    for k in range(1, seqs):
        other = lax.rem(sq + k, seqs)
        emb_copy(other).wait_send()
        arrived(emb_out.at[other], emb_recv.at[other])


def gather_all(stage, eq, eo, kw, vw):
    dps, seqs = lax.axis_size("dp"), lax.axis_size("seq")
    anywhere = pl.BlockSpec(memory_space=pl.ANY)
    dma = pltpu.SemaphoreType.DMA
    shape = jax.ShapeDtypeStruct
    return pl.pallas_call(
        functools.partial(gather_kernel, dps, seqs),
        out_shape=[shape(stage.shape, BF16)]
        + [shape((dps,) + w.shape, BF16) for w in (eq, eo, kw, vw)],
        in_specs=[anywhere] * 5,
        out_specs=[anywhere] * 5,
        scratch_shapes=[
            dma((4, dps)),
            dma((4, dps)),
            dma((4, dps)),
            dma((seqs,)),
            dma((seqs,)),
            dma((5,)),
        ],
        compiler_params=pltpu.CompilerParams(collective_id=0, has_side_effects=True),
    )(stage, eq, eo, kw, vw)


def nt(a, b):
    return lax.dot_general(a, b, (((1,), (1,)), ((), ())), preferred_element_type=F32)


def nn(a, b):
    return lax.dot_general(a, b, (((1,), (0,)), ((), ())), preferred_element_type=F32)


def tn(a, b):
    return lax.dot_general(a, b, (((0,), (0,)), ((), ())), preferred_element_type=F32)


def softmax_rows(scores):
    top = jnp.max(scores, axis=-1, keepdims=True)
    expo = jnp.exp(scores - top)
    return expo / jnp.sum(expo, axis=-1, keepdims=True)


def math_kernel(
    nbr,
    embt,
    mem,
    gq,
    gc,
    eqw,
    eow,
    kw,
    vw,
    ctx_out,
    grad_out,
    mem_out,
    emb,
    eq,
    att,
    probs_buf,
    keys,
    values,
    dkeys,
    dvalues,
):
    count = mem.shape[0] // BLOCK
    width = eqw.shape[0]
    enc_heads = width // HEAD
    heads = kw.shape[1] // HEAD
    emb[...] = embt[...].T
    eq[...] = nn(emb[...], eqw[...]).astype(BF16)
    for h in range(enc_heads):
        cols = slice(h * HEAD, (h + 1) * HEAD)
        vcols = slice(width + h * HEAD, width + (h + 1) * HEAD)
        for b in range(count):
            rows = slice(b * nbr, (b + 1) * nbr)
            toks = slice(b * BLOCK, (b + 1) * BLOCK)
            probs = softmax_rows(nt(eq[rows, cols], mem[toks, cols]) * SCALE)
            probs_buf[h * count + b] = probs
            att[rows, cols] = nn(probs.astype(BF16), mem[toks, vcols]).astype(BF16)
    encoded = (emb[...].astype(F32) + nn(att[...], eow[...])).astype(BF16)
    keys[...] = nn(encoded, kw[...]).astype(BF16)
    values[...] = nn(encoded, vw[...]).astype(BF16)

    def head(h, carry):
        cols = pl.ds(pl.multiple_of(h * HEAD, HEAD), HEAD)
        for b in range(count):
            rows = slice(b * nbr, (b + 1) * nbr)
            toks = slice(b * BLOCK, (b + 1) * BLOCK)
            q, g, k, v = gq[toks, cols], gc[toks, cols], keys[rows, cols], values[rows, cols]
            probs = softmax_rows(nt(q, k) * SCALE)
            weights = probs.astype(BF16)
            ctx_out[toks, cols] = nn(weights, v).astype(BF16)
            d_probs = nt(g, v)
            centred = d_probs - jnp.sum(probs * d_probs, axis=-1, keepdims=True)
            d_scores = (probs * centred * SCALE).astype(BF16)
            grad_out[toks, cols] = nn(d_scores, k).astype(BF16)
            dkeys[rows, cols] = tn(d_scores, q).astype(BF16)
            dvalues[rows, cols] = tn(weights, g).astype(BF16)
        return carry

    lax.fori_loop(0, heads, head, 0, unroll=4)
    enc_grad = (nt(dkeys[...], kw[...]) + nt(dvalues[...], vw[...])).astype(BF16)
    att[...] = nt(enc_grad, eow[...]).astype(BF16)
    for h in range(enc_heads):
        cols = slice(h * HEAD, (h + 1) * HEAD)
        vcols = slice(width + h * HEAD, width + (h + 1) * HEAD)
        for b in range(count):
            rows = slice(b * nbr, (b + 1) * nbr)
            toks = slice(b * BLOCK, (b + 1) * BLOCK)
            probs = probs_buf[h * count + b]
            grad = att[rows, cols]
            inner = nt(grad, mem[toks, vcols])
            centred = inner - jnp.sum(probs * inner, axis=-1, keepdims=True)
            d_scores = (probs * centred * SCALE).astype(BF16)
            mem_out[toks, cols] = tn(d_scores, eq[rows, cols]).astype(BF16)
            mem_out[toks, vcols] = tn(probs.astype(BF16), grad).astype(BF16)


def math_all(nbr, embt, mem, gq, gc, eqw, eow, kw, vw):
    width, tokens = embt.shape
    count = mem.shape[0] // BLOCK
    wide = kw.shape[1]
    vmem = pl.BlockSpec(memory_space=pltpu.VMEM)
    shape = jax.ShapeDtypeStruct
    return pl.pallas_call(
        functools.partial(math_kernel, nbr),
        out_shape=[shape(gq.shape, BF16), shape(gq.shape, BF16), shape(mem.shape, BF16)],
        in_specs=[vmem] * 8,
        out_specs=[vmem] * 3,
        scratch_shapes=[
            pltpu.VMEM((tokens, width), BF16),
            pltpu.VMEM((tokens, width), BF16),
            pltpu.VMEM((tokens, width), BF16),
            pltpu.VMEM((width // HEAD * count, nbr, BLOCK), F32),
        ]
        + [pltpu.VMEM((tokens, wide), BF16)] * 4,
    )(embt, mem, gq, gc, eqw, eow, kw, vw)


def body(
    queries,
    block_memory,
    neighbour_ids,
    embedding,
    enc_query_w,
    enc_out_w,
    key_w,
    value_w,
    context_cot,
):
    q, mem, ids, cot = queries[0], block_memory[0], neighbour_ids[0], context_cot[0]
    tokens, wide = q.shape
    nbr = ids.shape[1]
    seqs = lax.axis_size("seq")
    all_ids, halo_q, halo_c = share_ids(q, cot, ids)
    stage = look_up(all_ids, embedding)
    emb, *gathered = gather_all(stage, enc_query_w, enc_out_w, key_w, value_w)
    flat = [w.reshape(-1, w.shape[2]) for w in gathered]
    last = lax.axis_index("seq") == seqs - 1
    halo_q = jnp.where(last, jnp.zeros_like(halo_q), halo_q)
    halo_c = jnp.where(last, jnp.zeros_like(halo_c), halo_c)
    gq = jnp.concatenate([q[BLOCK - 1 :], halo_q[: BLOCK - 1]], axis=0)
    gc = jnp.concatenate([cot[BLOCK - 1 :], halo_c[: BLOCK - 1]], axis=0)
    ctx, grad, mem_grad = math_all(nbr, emb.reshape(-1, emb.shape[2]), mem, gq, gc, *flat)
    ring = [(s, s + 1) for s in range(seqs - 1)]
    back_c = lax.ppermute(ctx[tokens - BLOCK :], "seq", ring)
    back_q = lax.ppermute(grad[tokens - BLOCK :], "seq", ring)
    context = jnp.concatenate([back_c[1:], ctx[: tokens - BLOCK + 1]], axis=0)
    query_grad = jnp.concatenate([back_q[1:], grad[: tokens - BLOCK + 1]], axis=0)
    return (context[None], query_grad[None], mem_grad[None])


def solution(mesh):
    rows = P("dp", "seq", None)
    split = P("dp", None)
    return jax.shard_map(
        body,
        mesh=mesh,
        in_specs=(rows, rows, rows, P("seq", None), split, split, split, split, rows),
        out_specs=(rows, rows, rows),
        check_vma=False,
    )
```

time: 264 us -> 189 us (0.72)
  Pallas kernels: 0 us -> 173 us
  waiting for transfers between devices: 97.8 us -> 0.01 us
  matrix products: 66.3 us -> 0 us
  local copies, waits for them, and re-layouts: 50.5 us -> 6.1 us
  blocking collectives: 13.6 us -> 0 us
  between operations: 14.2 us -> 0.74 us
  starting transfers between devices: 12.3 us -> 4.7 us
  other arithmetic: 7.63 us -> 3.53 us
    pallas_call x0 -> x4, Pallas kernels: none -> 173 us  [the longest x1 83.4 us: gather_all(): pl.pallas_call(functools.partial(gather_kernel, dps, seqs), out_shape=[sh...]
    all_gather x4 -> x0, waiting for transfers between devices: 89.3 us -> none  [the longest x1 46.4 us: body(): lax.all_gather(key_w, 'dp', axis=0, tiled=True)]
    dot_general x17 -> x0, matrix products: 66.3 us -> none  [the longest x1 14.1 us: attend_grad(): jnp.einsum('chtn,cnhd->cthd', d_scores, group_k, preferred_element_type=j...]
    unnamed x43 -> x4, local copies, waits for them, and re-layouts: 23.4 us -> 0.01 us
    gather x2 -> x0, local copies, waits for them, and re-layouts: 13.6 us -> none  [body(): looked = jnp.take(embedding, all_ids.reshape(-1), axis=1)]
    all_gather x1 -> x0, blocking collectives: 13.6 us -> none  [body(): all_ids = lax.all_gather(neighbour_ids, 'seq', axis=1, tiled=True)[0]]
    convert_element_type x6 -> x0, local copies, waits for them, and re-layouts: 6.37 us -> none  [the longest x1 1.68 us: body(): key_b = key_sum.astype(jnp.bfloat16).reshape(count * nbr, width)]
    all_to_all x1 -> x0, waiting for transfers between devices: 5.59 us -> none  [body(): lax.all_to_all(looked, 'seq', split_axis=1, concat_axis=0, tiled=True)]
  transfers between devices with their start and end apart: 9 -> 2, of which waited for: 4 -> 0; matrix products, arithmetic and copies ran while one was open for 29% -> 2% of each run, Pallas kernels for 0% -> 0%
where the time goes in v1:
time: 189 us; the launch traced here: 188 us
  Pallas kernels  173 us (92%)
  local copies, waits for them, and re-layouts  6.1 us (3%)
  starting transfers between devices  4.7 us (2%)
  other arithmetic  3.53 us (2%)
    pallas_call x1, Pallas kernels, gather_all(): pl.pallas_call(functools.partial(gather_kernel, dps, seqs), out_shape=[sh...  83.4 us
    pallas_call x1, Pallas kernels, look_up(): pl.pallas_call(look_kernel, out_shape=jax.ShapeDtypeStruct((seqs, feats,...  40.3 us
    pallas_call x1, Pallas kernels, math_all(): pl.pallas_call(functools.partial(math_kernel, nbr), out_shape=[shape(gq.s...  36.8 us
    pallas_call x1, Pallas kernels, share_ids(): pl.pallas_call(functools.partial(ids_kernel, seqs), out_shape=[shape((seq...  12.5 us
  transfers between devices with their start and end apart: 2, of which 0 were waited for; matrix products, arithmetic and copies ran while one was open for 2% of the time, Pallas kernels for 0%

profile of v1, /device:TPU:0, one launch (start us, length us, event | category | flops | bytes accessed | tf_op | source)
XLA Modules:
  0.0 188.1 jit_solution(11084425733964397506)
XLA Ops:
  0.6 1.0 slice_bitcast_fusion.1
  1.7 1.0 slice_bitcast_fusion
  2.7 12.5 %shard_map.112 = (s32[8,2,128]{2,1,0:T(2,128)}, bf16[64,2048]{1,0:T(8,128)(2,1)}, bf16[64,2048]{1,0:T(8,128)(2,1)}) custom-call(bf16[128,2048]{1,0:T(8,128)(2,1)} %bitcast.22, bf16[128,2048]{1,0:T(8,128)(2,1)} %bitcast.23, s32[2,128]{1,0:T(2,128)} %bitcast.26), custom_call_target="tpu_custom_call" | custom-call | tf_op jit(solution)/shard_map/pallas_call | solution.py:65
  15.2 0.0 copy-start
  15.3 0.0 copy-start.1
  15.3 40.3 %shard_map.113.stage = bf16[8,112,256]{2,1,0:T(8,128)(2,1)} custom-call(s32[8,2,128]{2,1,0:T(2,128)} %get-tuple-element.14.ids, bf16[112,64000]{1,0:T(8,128)(2,1)} %table.1), custom_call_target="tpu_custom_call" | custom-call | tf_op jit(solution)/shard_map/pallas_call | solution.py:110
  55.6 0.0 copy-done
  55.6 0.0 copy-done.1
  55.7 0.9 pad_maximum_fusion.1.gc
  56.5 0.9 pad_maximum_fusion.gq
  57.4 83.4 %shard_map.114 = (bf16[8,112,256]{2,1,0:T(8,128)(2,1)}, bf16[4,224,896]{2,1,0:T(8,128)(2,1)}, bf16[4,224,896]{2,1,0:T(8,128)(2,1)}, bf16[4,224,2048]{2,1,0:T(8,128)(2,1)}, bf16[4,224,2048]{2,1,0:T(8,128)(2,1)}) custom-call(bf16[8,112,256]{2,1,0:T(8,128)(2,1)} %shard_map.113.stage, bf16[224,896]{1,0:T(8,128)(2,1)} %eq_ref.1, bf16[224,896]{1,0:T(8,128)(2,1)} %eo_ref.1, ...), custom_call_target="tpu_custom_call" | custom-call | tf_op jit(solution)/shard_map/pallas_call | solution.py:240
  140.8 36.8 %shard_map.115 = (bf16[128,2048]{1,0:T(8,128)(2,1)}, bf16[128,2048]{1,0:T(8,128)(2,1)}, bf16[128,1792]{1,0:T(8,128)(2,1)}) custom-call(bf16[896,256]{1,0:T(8,128)(2,1)} %bitcast.25, bf16[128,1792]{1,0:T(8,128)(2,1)} %bitcast.24, bf16[128,2048]{1,0:T(8,128)(2,1)} %pad_maximum_fusion.gq, bf16[128,2048]{1,0:T(8,128)(2,1)} %pad_maximum_fusion.1.gc, ...), custom_call_target="tpu_custom_call" | custom-call | tf_op jit(solution)/shard_map/pallas_call | solution.py:358
  177.6 1.0 slice.45
  178.5 2.8 %collective-permute-start.1 = (bf16[64,2048]{1,0:T(8,128)(2,1)S(1)}, bf16[64,2048]{1,0:T(8,128)(2,1)S(1)}, u32[]{:S(2)}, u32[]{:S(2)}) collective-permute-start(bf16[64,2048]{1,0:T(8,128)(2,1)S(1)} %slice.45), channel_id=1, source_target_pairs={{0,1},{1,2},{2,3},{3,4},{4,5},{5,6},{6,7},{8,9},{9,10},{10,11},{11... | collective-permute-start | bytes 786440 | tf_op jit(solution)/shard_map/ppermute | solution.py:400
  181.3 1.0 slice.42
  182.3 1.9 %collective-permute-start = (bf16[64,2048]{1,0:T(8,128)(2,1)S(1)}, bf16[64,2048]{1,0:T(8,128)(2,1)S(1)}, u32[]{:S(2)}, u32[]{:S(2)}) collective-permute-start(bf16[64,2048]{1,0:T(8,128)(2,1)S(1)} %slice.42), channel_id=1, source_target_pairs={{0,1},{1,2},{2,3},{3,4},{4,5},{5,6},{6,7},{8,9},{9,10},{10,11},{11... | collective-permute-start | bytes 786440 | tf_op jit(solution)/shard_map/ppermute | solution.py:399
  184.2 1.0 slice.44
  185.2 1.0 slice.47
  186.2 0.0 collective-permute-done.1
  186.2 0.1 slice.51
  186.3 0.9 maximum_bitcast_fusion.1
  187.1 0.0 collective-permute-done
  187.1 0.1 slice.50
  187.2 0.9 maximum_bitcast_fusion
  (1 shorter events, 0.0 us)
Async XLA Ops:
  15.2 40.4 %copy-start = (bf16[64,2048]{1,0:T(8,128)(2,1)S(1)}, bf16[64,2048]{1,0:T(8,128)(2,1)}, u32[]{:S(2)}) copy-start(bf16[64,2048]{1,0:T(8,128)(2,1)} %get-tuple-element.16) | copy-start | bytes 786436
  15.3 40.4 %copy-start.1 = (bf16[64,2048]{1,0:T(8,128)(2,1)S(1)}, bf16[64,2048]{1,0:T(8,128)(2,1)}, u32[]{:S(2)}) copy-start(bf16[64,2048]{1,0:T(8,128)(2,1)} %get-tuple-element.17) | copy-start | bytes 786436
  178.5 7.7 %collective-permute-start.1 = (bf16[64,2048]{1,0:T(8,128)(2,1)S(1)}, bf16[64,2048]{1,0:T(8,128)(2,1)S(1)}, u32[]{:S(2)}, u32[]{:S(2)}) collective-permute-start(bf16[64,2048]{1,0:T(8,128)(2,1)S(1)} %slice.45), channel_id=1, source_target_pairs={{0,1},{1,2},{2,3},{3,4},{4,5},{5,6},{6,7},{8,9},{9,10},{10,11},{11... | collective-permute-start | bytes 786440 | tf_op jit(solution)/shard_map/ppermute | solution.py:400
  182.3 4.9 %collective-permute-start = (bf16[64,2048]{1,0:T(8,128)(2,1)S(1)}, bf16[64,2048]{1,0:T(8,128)(2,1)S(1)}, u32[]{:S(2)}, u32[]{:S(2)}) collective-permute-start(bf16[64,2048]{1,0:T(8,128)(2,1)S(1)} %slice.42), channel_id=1, source_target_pairs={{0,1},{1,2},{2,3},{3,4},{4,5},{5,6},{6,7},{8,9},{9,10},{10,11},{11... | collective-permute-start | bytes 786440 | tf_op jit(solution)/shard_map/ppermute | solution.py:399
